TPU v7x, 32 devices: a whole 2x2x4 slice. The times are simulated.
32 devices in a mesh: tp: 8 (over y, x, core), dp: 4 (over z).
Axes of the slice: x: 2, y: 2, z: 4, core: 2. Of those that a mesh axis runs over, the one named last changes fastest.
Arguments:
- activations: bfloat16 [64, 512, 4096], P('dp', None, 'tp'), may hold values from -6 to 6
- query_output_cotangent: bfloat16 [64, 512, 4096], P('dp', None, 'tp'), may hold values from -6 to 6
- value_output_cotangent: bfloat16 [64, 512, 4096], P('dp', None, 'tp'), may hold values from -6 to 6
- lengths: int32 [64], P('dp'), may hold values from 1 to 512
- reducing_matrices_pair: bfloat16 [2, 4096, 128], P(None, 'tp'), may hold values from -0.09375 to 0.09375
- expanding_matrices_pair: bfloat16 [2, 128, 4096], P(None, None, 'tp'), may hold values from -0.5 to 0.5
- width_side_projections: bfloat16 [2, 4096, 128], P(None, 'tp'), may hold values from -0.09375 to 0.09375
- narrow_random_sketch: bfloat16 [128, 16], replicated, may hold values from -0.5 to 0.5
- projected_first_moment: float32 [8192], replicated, may hold values from -6 to 6
- projected_second_moment: float32 [8192], replicated, may hold values from 0.1 to 10
- targets: bfloat16 [1024, 8192], P('dp', 'tp'), may hold values from -6 to 6
Outputs:
- scores: float32 [64, 1024], P('dp', 'tp')
All inputs are finite; a program needn't handle non-finite values.
Results may differ from a plain program's by a relative error of at most 0.023.
Values may be sent and summed in bfloat16 or wider, within the bound.
A program may use at most 128 MiB of HBM per device.

v0:
```python
import math

import jax
import jax.numpy as jnp
from jax import lax
from jax.sharding import PartitionSpec as P


def compute_features(token_sums, token_mask, layout, rank_cols):
    wide_cols = (token_sums.shape[-1] - 4 * rank_cols) // 3
    bounds = [
        0,
        rank_cols,
        2 * rank_cols,
        2 * rank_cols + wide_cols,
        3 * rank_cols + wide_cols,
        3 * rank_cols + 2 * wide_cols,
        4 * rank_cols + 2 * wide_cols,
        4 * rank_cols + 3 * wide_cols,
    ]
    pieces = [token_sums[..., bounds[i] : bounds[i + 1]] for i in range(7)]
    down_q, down_v, input_side, back_q, output_q, back_v, output_v = pieces
    weights = token_mask[..., None]
    pattern = layout + "r," + layout + "k->erk"

    def outer_sum(left_side, right_side):
        return jnp.einsum(pattern, left_side, right_side, precision=lax.Precision.HIGHEST)

    stacked = jnp.stack(
        [
            outer_sum(back_q * weights, input_side),
            outer_sum(back_v * weights, input_side),
            outer_sum(down_q * weights, output_q),
            outer_sum(down_v * weights, output_v),
        ],
        axis=1,
    )
    return stacked.reshape(stacked.shape[0], -1)


def adam_update(features, first_moment, second_moment):
    mixed = 0.9 * first_moment + 0.1 * features
    spread = 0.999 * second_moment + 0.001 * features * features
    return mixed / (jnp.sqrt(spread) + 1e-08)


def combine_factors(reducing_matrices_pair, expanding_matrices_pair, narrow_random_sketch):
    attention_key_reducer = jnp.dot(
        reducing_matrices_pair[0], narrow_random_sketch, preferred_element_type=jnp.float32
    ).astype(jnp.bfloat16)
    value_down_factor = jnp.dot(
        reducing_matrices_pair[1], narrow_random_sketch, preferred_element_type=jnp.float32
    ).astype(jnp.bfloat16)
    query_up_factor = jnp.dot(
        expanding_matrices_pair[0].T, narrow_random_sketch, preferred_element_type=jnp.float32
    ).astype(jnp.bfloat16)
    value_up_factor = jnp.dot(
        expanding_matrices_pair[1].T, narrow_random_sketch, preferred_element_type=jnp.float32
    ).astype(jnp.bfloat16)
    return (attention_key_reducer, value_down_factor, query_up_factor, value_up_factor)


def body(
    activations,
    query_output_cotangent,
    value_output_cotangent,
    lengths,
    reducing_matrices_pair,
    expanding_matrices_pair,
    width_side_projections,
    narrow_random_sketch,
    projected_first_moment,
    projected_second_moment,
    targets,
):
    attention_key_reducer, value_down_factor, query_up_factor, value_up_factor = combine_factors(
        reducing_matrices_pair, expanding_matrices_pair, narrow_random_sketch
    )
    rank_cols = narrow_random_sketch.shape[1]
    w_left = jnp.concatenate(
        [attention_key_reducer, value_down_factor, width_side_projections[0]], axis=1
    )
    w_query = jnp.concatenate([query_up_factor, width_side_projections[1]], axis=1)
    w_value = jnp.concatenate([value_up_factor, width_side_projections[1]], axis=1)
    groups = lax.axis_size("tp")
    member = lax.axis_index("tp")
    local_ex = activations.shape[0]
    seq_len = activations.shape[1]
    feature_count = projected_first_moment.shape[0]
    positions = jnp.arange(seq_len, dtype=jnp.int32)
    token_mask = (positions[None, :] < lengths[:, None]).astype(jnp.float32)
    target_float = targets.astype(jnp.float32)
    target_sq = jnp.sum(target_float * target_float, axis=1)
    own_rows = local_ex // groups
    left_part = jnp.einsum("esd,dc->esc", activations, w_left, preferred_element_type=jnp.float32)
    right_q = jnp.einsum(
        "esd,dc->esc", query_output_cotangent, w_query, preferred_element_type=jnp.float32
    )
    right_v = jnp.einsum(
        "esd,dc->esc", value_output_cotangent, w_value, preferred_element_type=jnp.float32
    )
    token_sums = lax.psum_scatter(
        jnp.concatenate([left_part, right_q, right_v], axis=-1).astype(jnp.bfloat16),
        "tp",
        scatter_dimension=0,
        tiled=True,
    ).astype(jnp.float32)
    own_mask = lax.dynamic_slice_in_dim(token_mask, member * own_rows, own_rows, 0)
    features = compute_features(token_sums, own_mask, "es", rank_cols)
    update = adam_update(features, projected_first_moment, projected_second_moment)
    squares = jnp.sum(update * update, axis=1)
    target_total = lax.psum(target_sq, "tp")
    own_train = (update * lax.rsqrt(squares + 1e-06)[:, None]).astype(jnp.bfloat16)
    train_rows = lax.all_to_all(own_train, "tp", split_axis=1, concat_axis=0, tiled=True)
    unit_targets = (target_float * lax.rsqrt(target_total + 1e-06)[:, None]).astype(jnp.bfloat16)
    partial_scores = lax.dot_general(
        train_rows,
        lax.all_gather(unit_targets, "dp", axis=0, tiled=True),
        (((1,), (1,)), ((), ())),
        preferred_element_type=jnp.float32,
    )
    scores = lax.psum_scatter(
        partial_scores.astype(jnp.bfloat16), "tp", scatter_dimension=1, tiled=True
    ).astype(jnp.float32)
    return scores * math.sqrt(feature_count)


def solution(mesh):
    placed = (
        P("dp", None, "tp"),
        P("dp", None, "tp"),
        P("dp", None, "tp"),
        P("dp"),
        P(None, "tp", None),
        P(None, None, "tp"),
        P(None, "tp", None),
        P(),
        P(),
        P(),
        P("dp", "tp"),
    )
    return jax.shard_map(body, mesh=mesh, in_specs=placed, out_specs=P("dp", "tp"), check_vma=False)
```

profile of v0, /device:TPU:0, one launch (start us, length us, event | category | flops | bytes accessed | tf_op | source)
XLA Modules:
  0.0 158.5 jit_solution(14947241364090054816)
XLA Ops:
  7.4 0.0 copy-start
  7.4 0.0 reduce-scatter.5.cloned.1.call-start
  7.4 0.7 copy-done
  8.1 1.0 convolution_convert_fusion.1
  9.1 1.0 convolution_convert_fusion.2
  10.1 1.0 convolution_convert_fusion.3
  11.2 1.1 convolution_convert_fusion.4
  12.2 1.0 fusion.41
  13.2 0.1 copy.41
  13.4 0.1 copy.40
  13.5 0.0 copy-start.1
  13.5 6.4 %convert_bitcast_fusion.1 = bf16[16,512,144]{1,2,0:T(8,128)(2,1)S(1)} fusion(bf16[16,512,512]{2,1,0:T(8,128)(2,1)} %param.13, bf16[512,16]{0,1:T(8,128)(2,1)S(1)} %convolution_convert_fusion.1, bf16[512,128]{0,1:T(8,128)(2,1)S(1)} %bitcast.53), kind=kOutput, calls=%fused_computation.2 | convolution fusion | flops 1209434112 | bytes 10895360 | tf_op jit(solution)/shard_map/esd,dc->esc/dot_general | solution.py:99
  19.9 0.0 copy-done.1
  19.9 0.0 copy-start.2
  19.9 2.9 %convert_bitcast_fusion.2 = bf16[16,512,144]{1,2,0:T(8,128)(2,1)S(1)} fusion(bf16[16,512,512]{2,1,0:T(8,128)(2,1)S(1)} %copy-done.1, bf16[512,16]{0,1:T(8,128)(2,1)S(1)} %convolution_convert_fusion.2, bf16[512,128]{0,1:T(8,128)(2,1)S(1)} %bitcast.54), kind=kOutput, calls=%fused_computation.3 | convolution fusion | flops 1209434112 | bytes 10895360 | tf_op jit(solution)/shard_map/esd,dc->esc/dot_general | solution.py:96
  22.8 0.5 copy-done.2
  23.3 2.9 %convert_bitcast_fusion = bf16[16,512,160]{1,2,0:T(8,128)(2,1)S(1)} fusion(bf16[16,512,512]{2,1,0:T(8,128)(2,1)S(1)} %copy-done.2, bf16[512,128]{0,1:T(8,128)(2,1)S(1)} %bitcast.56, bf16[512,16]{0,1:T(8,128)(2,1)S(1)} %convolution_convert_fusion.3, bf16[512,16]{0,1:T(8,128)(2,1)S(1)} %convolution_convert_fusion.4), kind=kOutput, calls=%fused_computation.1 | convolution fusion | flops 1343979520 | bytes 11173888 | tf_op jit(solution)/shard_map/esd,dc->esc/dot_general | solution.py:95
  26.2 3.4 %pad_maximum_fusion = bf16[16,512,448]{1,2,0:T(8,128)(2,1)} fusion(bf16[16,512,144]{1,2,0:T(8,128)(2,1)S(1)} %convert_bitcast_fusion.1, bf16[16,512,144]{1,2,0:T(8,128)(2,1)S(1)} %convert_bitcast_fusion.2, bf16[16,512,160]{1,2,0:T(8,128)(2,1)S(1)} %convert_bitcast_fusion), kind=kLoop, calls=%fused_computation | loop fusion | flops 22020096 | bytes 14680064 | tf_op jit(solution)/shard_map/concatenate | solution.py:103
  29.5 0.0 copy-start.3
  29.5 0.0 reduce-scatter.5.cloned.1.call-update
  29.6 0.0 all-gather.2.cloned.1.call-start
  29.6 1.0 copy-done.3
  30.6 0.2 fusion
  30.7 15.1 %psum.7 = f32[256]{0:T(256)S(1)} all-reduce(f32[256]{0:T(256)S(1)} %fusion), channel_id=1, replica_groups=mesh['tp'=8,'dp'=4] {'tp'}, use_global_device_ids=true, to_apply=%region_3.0 | all-reduce | flops 256 | bytes 2048 | tf_op jit(solution)/shard_map/psum | solution.py:112
  45.9 1.0 fusion.1
  46.8 0.0 all-gather.2.cloned.1.call-update
  46.9 0.0 reduce-scatter.7.cloned.1.call-start
  46.9 0.0 copy-done.4
  47.0 0.0 copy-done.5
  47.0 0.0 copy-done.6
  47.0 0.1 dynamic-slice
  47.1 0.1 compare_convert_fusion
  47.2 52.2 %reduce-scatter.5.cloned.1.call-done = bf16[2,512,448]{1,2,0:T(8,128)(2,1)} async-done(((bf16[16,512,448]{1,2,0:T(8,128)(2,1)}), bf16[2,512,448]{1,2,0:T(8,128)(2,1)}) %reduce-scatter.5.cloned.1.call-update) | async-done | bytes 917520 | tf_op jit(solution)/shard_map/reduce_scatter | solution.py:102
  99.3 1.4 convert_element_type.39
  100.8 1.3 convolution_bitcast_fusion.3
  102.0 1.3 convolution_bitcast_fusion.2
  103.3 1.3 convolution_bitcast_fusion.1
  104.6 1.3 convolution_bitcast_fusion
  105.8 0.2 fusion.33
  106.0 0.1 fusion.32
  106.2 7.4 %all_to_all.16 = bf16[2,8,1024]{2,0,1:T(2,128)(2,1)S(1)} all-to-all(bf16[2,8,1024]{2,0,1:T(2,128)(2,1)S(1)} %copy.33), channel_id=1, replica_groups=mesh['tp'=8,'dp'=4] {'tp'}, dimensions={1} | all-to-all | bytes 65536 | tf_op jit(solution)/shard_map/all_to_all | solution.py:114
  113.6 0.0 all-gather.2.cloned.1.call-done
  113.6 2.2 %convolution_convert_fusion = bf16[16,1024]{1,0:T(8,128)(2,1)S(1)} fusion(bf16[16,1024]{1,0:T(8,128)(2,1)S(1)} %all_to_all.14, bf16[1024,1024]{1,0:T(8,128)(2,1)} %all-gather.2.cloned.1.call-done), kind=kOutput, calls=%fused_computation.6 | convolution fusion | flops 33570816 | bytes 2162688 | tf_op jit(solution)/shard_map/dot_general | solution.py:116
  115.8 0.8 copy.38
  116.7 0.0 reduce-scatter.7.cloned.1.call-update
  116.7 32.9 %reduce-scatter.7.cloned.1.call-done = bf16[128,16]{1,0:T(8,128)(2,1)} async-done(((bf16[1024,16]{1,0:T(8,128)(2,1)}), bf16[128,16]{1,0:T(8,128)(2,1)}) %reduce-scatter.7.cloned.1.call-update) | async-done | bytes 4112
  149.6 0.8 copy.39
  150.4 0.6 convert_multiply_fusion.2
  (13 shorter events, 0.1 us)
Async XLA Ops:
  7.4 0.7 copy-start
  7.4 92.0 %reduce-scatter.5.cloned.1.call-start = ((), (), s32[]{:S(2)}) async-start(), calls=%async_computation.3 | async-start | bytes 8257536 | tf_op jit(solution)/shard_map/reduce_scatter | solution.py:102
  13.5 6.4 %copy-start.1 = (bf16[16,512,512]{2,1,0:T(8,128)(2,1)S(1)}, bf16[16,512,512]{2,1,0:T(8,128)(2,1)}, u32[]{:S(2)}) copy-start(bf16[16,512,512]{2,1,0:T(8,128)(2,1)} %param.12) | copy-start | bytes 25165828
  19.9 3.4 %copy-start.2 = (bf16[16,512,512]{2,1,0:T(8,128)(2,1)S(1)}, bf16[16,512,512]{2,1,0:T(8,128)(2,1)}, u32[]{:S(2)}) copy-start(bf16[16,512,512]{2,1,0:T(8,128)(2,1)} %param.11) | copy-start | bytes 25165828
  29.5 1.0 copy-start.3
  29.5 17.4 %copy-start.4 = (f32[8192]{0:T(1024)S(1)}, f32[8192]{0:T(1024)}, u32[]{:S(2)}) copy-start(f32[8192]{0:T(1024)} %param.19) | copy-start | bytes 98308
  29.5 17.4 %copy-start.5 = (f32[8192]{0:T(1024)S(1)}, f32[8192]{0:T(1024)}, u32[]{:S(2)}) copy-start(f32[8192]{0:T(1024)} %param.20) | copy-start | bytes 98308
  29.5 17.5 %copy-start.6 = (s32[16]{0:T(128)S(1)}, s32[16]{0:T(128)}, u32[]{:S(2)}) copy-start(s32[16]{0:T(128)} %param.14) | copy-start | bytes 196
  29.6 84.0 %all-gather.2.cloned.1.call-start = ((), (), s32[]{:S(2)}) async-start(), calls=%async_computation.4 | async-start | bytes 2621440 | tf_op jit(solution)/shard_map/all_gather | solution.py:118
  46.9 102.7 %reduce-scatter.7.cloned.1.call-start = ((), (), s32[]{:S(2)}) async-start(), calls=%async_computation.5 | async-start | bytes 294912
Sparse Core Ops, SparseCore 0:
  29.7 69.6 reduce-scatter.4
  116.8 32.7 reduce-scatter.6
Sparse Core Ops, SparseCore 1:
  47.0 44.9 all-gather.1
where the time goes:
time: 159 us; the launch traced here: 158 us
  waiting for transfers between devices  85.1 us (54%)
  matrix products  23.6 us (15%)
  blocking collectives  22.5 us (14%)
  between operations  15 us (9%)
  other arithmetic  6.89 us (4%)
  local copies, waits for them, and re-layouts  5.24 us (3%)
    reduce_scatter x1, waiting for transfers between devices, body(): lax.psum_scatter(jnp.concatenate([left_part, right_q, right_v], axis=-1)....  52.2 us
    unnamed x4, waiting for transfers between devices  32.9 us
    psum x1, blocking collectives, body(): target_total = lax.psum(target_sq, 'tp')  15.1 us
    all_to_all x1, blocking collectives, body(): lax.all_to_all(own_train, 'tp', split_axis=1, concat_axis=0, tiled=True)  7.37 us
    dot_general x1, matrix products, body(): jnp.einsum('esd,dc->esc', value_output_cotangent, w_value, preferred_elem...  6.4 us
    dot_general x4, matrix products, outer_sum(): jnp.einsum(pattern, left_side, right_side, precision=lax.Precision.HIGHEST)  5.09 us
    unnamed x18, local copies, waits for them, and re-layouts  4.05 us
    concatenate x1, other arithmetic, body(): jnp.concatenate([left_part, right_q, right_v], axis=-1).astype(jnp.bfloat16)  3.35 us
  transfers between devices with their start and end apart: 3, of which 2 were waited for; matrix products, arithmetic and copies ran while one was open for 5% of the time, Pallas kernels for 0%

commit v1 on v0

v1 whole, which is shorter than its diff:
```python
import math

import jax
import jax.numpy as jnp
from jax import lax
from jax.sharding import PartitionSpec as P


def adam_update(features, first_moment, second_moment):
    mixed = 0.9 * first_moment + 0.1 * features
    spread = 0.999 * second_moment + 0.001 * features * features
    return mixed / (jnp.sqrt(spread) + 1e-08)


def combine_factors(reducing_matrices_pair, expanding_matrices_pair, narrow_random_sketch):
    attention_key_reducer = jnp.dot(
        reducing_matrices_pair[0], narrow_random_sketch, preferred_element_type=jnp.float32
    ).astype(jnp.bfloat16)
    value_down_factor = jnp.dot(
        reducing_matrices_pair[1], narrow_random_sketch, preferred_element_type=jnp.float32
    ).astype(jnp.bfloat16)
    query_up_factor = jnp.dot(
        expanding_matrices_pair[0].T, narrow_random_sketch, preferred_element_type=jnp.float32
    ).astype(jnp.bfloat16)
    value_up_factor = jnp.dot(
        expanding_matrices_pair[1].T, narrow_random_sketch, preferred_element_type=jnp.float32
    ).astype(jnp.bfloat16)
    return (attention_key_reducer, value_down_factor, query_up_factor, value_up_factor)


def body(
    activations,
    query_output_cotangent,
    value_output_cotangent,
    lengths,
    reducing_matrices_pair,
    expanding_matrices_pair,
    width_side_projections,
    narrow_random_sketch,
    projected_first_moment,
    projected_second_moment,
    targets,
):
    attention_key_reducer, value_down_factor, query_up_factor, value_up_factor = combine_factors(
        reducing_matrices_pair, expanding_matrices_pair, narrow_random_sketch
    )
    rank_cols = narrow_random_sketch.shape[1]
    w_left = jnp.concatenate(
        [attention_key_reducer, value_down_factor, width_side_projections[0]], axis=1
    )
    w_query = jnp.concatenate([query_up_factor, width_side_projections[1]], axis=1)
    w_value = jnp.concatenate([value_up_factor, width_side_projections[1]], axis=1)
    groups = lax.axis_size("tp")
    parts = lax.axis_size("dp")
    member = lax.axis_index("tp")
    local_ex, seq_len = activations.shape[:2]
    feature_count = projected_first_moment.shape[0]
    positions = jnp.arange(seq_len, dtype=jnp.int32)
    token_mask = (positions[None, :] < lengths[:, None])[..., None]

    def project(rows, weights):
        out = jnp.einsum("esd,dc->esc", rows, weights, preferred_element_type=jnp.float32)
        return out.astype(jnp.bfloat16)

    left = project(activations, w_left)
    right_q = project(query_output_cotangent, w_query)
    right_v = project(value_output_cotangent, w_value)
    narrow = jnp.concatenate(
        [left[..., : 2 * rank_cols], right_q[..., :rank_cols], right_v[..., :rank_cols]], axis=-1
    )
    narrow = jnp.where(token_mask, narrow, jnp.zeros((), jnp.bfloat16))
    narrow = lax.psum(narrow, "tp")

    def outer_sum(first, wide):
        return jnp.einsum(
            "esr,esk->erk",
            narrow[..., first * rank_cols : (first + 1) * rank_cols],
            wide,
            preferred_element_type=jnp.float32,
        )

    own_features = jnp.concatenate(
        [
            outer_sum(2, left[..., 2 * rank_cols :]),
            outer_sum(3, left[..., 2 * rank_cols :]),
            outer_sum(0, right_q[..., rank_cols:]),
            outer_sum(1, right_v[..., rank_cols:]),
        ],
        axis=1,
    ).reshape(local_ex, -1)
    features = lax.psum_scatter(
        own_features.astype(jnp.bfloat16), "tp", scatter_dimension=1, tiled=True
    ).astype(jnp.float32)
    span = feature_count // groups
    first_moment = lax.dynamic_slice_in_dim(projected_first_moment, member * span, span)
    second_moment = lax.dynamic_slice_in_dim(projected_second_moment, member * span, span)
    update = adam_update(features, first_moment, second_moment).astype(jnp.bfloat16)
    update = lax.all_gather(update, "dp", axis=0, tiled=True)
    wide_update = update.astype(jnp.float32)
    target_float = targets.astype(jnp.float32)
    update_sq = jnp.sum(wide_update * wide_update, axis=1)
    target_sq = jnp.sum(target_float * target_float, axis=1)
    dots = lax.dot_general(
        update, targets, (((1,), (1,)), ((), ())), preferred_element_type=jnp.float32
    )
    rows = jnp.concatenate(
        [dots, jnp.broadcast_to(update_sq[:, None], (dots.shape[0], 128))], axis=1
    ).reshape(parts, local_ex, -1)
    extra = jnp.pad(target_sq, (0, 128))
    rows = jnp.concatenate([rows, jnp.broadcast_to(extra, (parts, 8, extra.shape[0]))], axis=1)
    rows = lax.psum(rows, "tp")
    rows = lax.all_to_all(rows, "dp", split_axis=0, concat_axis=0, tiled=True)
    owned = targets.shape[0]
    totals = jnp.moveaxis(rows[:, :, :owned], 0, 1).reshape(local_ex + 8, parts * owned)
    columns = parts * owned // groups
    totals = lax.dynamic_slice_in_dim(totals, member * columns, columns, 1)
    row_scale = lax.rsqrt(rows[0, :local_ex, owned : owned + 1] + 1e-06)
    column_scale = lax.rsqrt(totals[local_ex : local_ex + 1] + 1e-06)
    return totals[:local_ex] * row_scale * column_scale * math.sqrt(feature_count)


def solution(mesh):
    placed = (
        P("dp", None, "tp"),
        P("dp", None, "tp"),
        P("dp", None, "tp"),
        P("dp"),
        P(None, "tp", None),
        P(None, None, "tp"),
        P(None, "tp", None),
        P(),
        P(),
        P(),
        P("dp", "tp"),
    )
    return jax.shard_map(body, mesh=mesh, in_specs=placed, out_specs=P("dp", "tp"), check_vma=False)
```

time: 159 us -> 221 us (1.39)
  waiting for transfers between devices: 85.1 us -> 150 us
  blocking collectives: 22.5 us -> 13.5 us
  matrix products: 23.6 us -> 29.7 us
  starting transfers between devices: 0.09 us -> 4.69 us
    psum x0 -> x2, waiting for transfers between devices: none -> 111 us  [the longest x1 59.4 us: body(): narrow = lax.psum(narrow, 'tp')]
    unnamed x4 -> x3, waiting for transfers between devices: 32.9 us -> 0.05 us
    reduce_scatter x1, waiting for transfers between devices: 52.2 us -> 31.9 us  [body(): lax.psum_scatter(own_features.astype(jnp.bfloat16), 'tp', scatter_dimensi...]
    psum x1 -> x0, blocking collectives: 15.1 us -> none  [body(): target_total = lax.psum(target_sq, 'tp')]
    all_gather x0 -> x1, blocking collectives: none -> 13.5 us  [body(): update = lax.all_gather(update, 'dp', axis=0, tiled=True)]
    all_to_all x1 -> x0, blocking collectives: 7.37 us -> none  [body(): lax.all_to_all(own_train, 'tp', split_axis=1, concat_axis=0, tiled=True)]
    all_to_all x0 -> x1, waiting for transfers between devices: none -> 6.65 us  [body(): rows = lax.all_to_all(rows, 'dp', split_axis=0, concat_axis=0, tiled=True)]
    dot_general x8, matrix products: 19.5 us -> 25.6 us  [the longest x3 20.4 us: project(): jnp.einsum('esd,dc->esc', rows, weights, preferred_element_type=jnp.float32)]
  transfers between devices with their start and end apart: 3 -> 4, of which waited for: 2 -> 4; matrix products, arithmetic and copies ran while one was open for 5% -> 0% of each run, Pallas kernels for 0% -> 0%
where the time goes in v1:
time: 221 us; the launch traced here: 220 us
  waiting for transfers between devices  150 us (68%)
  matrix products  29.7 us (13%)
  blocking collectives  13.5 us (6%)
  between operations  13.3 us (6%)
  other arithmetic  4.71 us (2%)
  starting transfers between devices  4.69 us (2%)
  local copies, waits for them, and re-layouts  4.36 us (2%)
    psum x1, waiting for transfers between devices, body(): narrow = lax.psum(narrow, 'tp')  59.4 us
    psum x1, waiting for transfers between devices, body(): rows = lax.psum(rows, 'tp')  52 us
    reduce_scatter x1, waiting for transfers between devices, body(): lax.psum_scatter(own_features.astype(jnp.bfloat16), 'tp', scatter_dimensi...  31.9 us
    dot_general x3, matrix products, project(): jnp.einsum('esd,dc->esc', rows, weights, preferred_element_type=jnp.float32)  20.4 us
    all_gather x1, blocking collectives, body(): update = lax.all_gather(update, 'dp', axis=0, tiled=True)  13.5 us
    all_to_all x1, waiting for transfers between devices, body(): rows = lax.all_to_all(rows, 'dp', split_axis=0, concat_axis=0, tiled=True)  6.65 us
    dot_general x4, matrix products, outer_sum(): jnp.einsum('esr,esk->erk', narrow[..., first * rank_cols:(first + 1) * ra...  4.82 us
    all_to_all x1, starting transfers between devices, body(): rows = lax.all_to_all(rows, 'dp', split_axis=0, concat_axis=0, tiled=True)  4.6 us
  transfers between devices with their start and end apart: 4, of which 4 were waited for; matrix products, arithmetic and copies ran while one was open for 0% of the time, Pallas kernels for 0%

profile of v1, /device:TPU:0, one launch (start us, length us, event | category | flops | bytes accessed | tf_op | source)
XLA Modules:
  0.0 220.2 jit_solution(16352123582546980845)
XLA Ops:
  6.5 0.0 copy-start
  6.5 0.0 all-reduce.4.cloned.1.call-start
  6.5 0.7 copy-done
  7.2 1.0 convolution_convert_fusion.2
  8.3 1.1 convolution_convert_fusion.3
  9.3 1.0 convolution_convert_fusion.1
  10.4 1.0 convolution_convert_fusion
  11.4 1.0 fusion.55
  12.4 0.1 copy.37
  12.5 6.3 %convert_bitcast_fusion = bf16[16,512,160]{1,2,0:T(8,128)(2,1)S(1)} fusion(bf16[16,512,512]{2,1,0:T(8,128)(2,1)} %param.11, bf16[512,128]{0,1:T(8,128)(2,1)S(1)} %bitcast.53, bf16[512,16]{0,1:T(8,128)(2,1)S(1)} %convolution_convert_fusion.2, bf16[512,16]{0,1:T(8,128)(2,1)S(1)} %convolution_convert_fusion.3), kind=kOutput, calls=%fused_computation | convolution fusion | flops 1343979520 | bytes 11173888 | tf_op jit(solution)/shard_map/esd,dc->esc/dot_general | solution.py:62
  18.8 0.0 copy-start.1
  18.8 0.1 copy.38
  18.9 7.1 %convert_bitcast_fusion.2 = bf16[16,512,144]{1,2,0:T(8,128)(2,1)S(1)} fusion(bf16[16,512,512]{2,1,0:T(8,128)(2,1)} %param.12, bf16[512,16]{0,1:T(8,128)(2,1)S(1)} %convolution_convert_fusion.1, bf16[512,128]{0,1:T(8,128)(2,1)S(1)} %bitcast.49), kind=kOutput, calls=%fused_computation.2 | convolution fusion | flops 1209434112 | bytes 10895360 | tf_op jit(solution)/shard_map/esd,dc->esc/dot_general | solution.py:62
  26.0 0.0 copy-done.1
  26.0 0.0 copy-start.3
  26.1 0.0 copy-start.8
  26.1 0.0 slice-start
  26.1 7.1 %convert_bitcast_fusion.1 = bf16[16,512,144]{1,2,0:T(8,128)(2,1)S(1)} fusion(bf16[16,512,512]{2,1,0:T(8,128)(2,1)} %param.13, bf16[512,16]{0,1:T(8,128)(2,1)S(1)} %convolution_convert_fusion, bf16[512,128]{0,1:T(8,128)(2,1)S(1)} %bitcast.50), kind=kOutput, calls=%fused_computation.1 | convolution fusion | flops 1209434112 | bytes 10895360 | tf_op jit(solution)/shard_map/esd,dc->esc/dot_general | solution.py:62
  33.2 1.4 copy-done.5
  34.6 0.1 iota_compare_fusion
  34.7 1.3 maximum_select_fusion
  36.0 0.0 all-reduce.4.cloned.1.call-update
  36.0 0.0 reduce-scatter.2.cloned.1.call-start
  36.1 59.4 %all-reduce.4.cloned.1.call-done = bf16[16,512,64]{1,2,0:T(8,128)(2,1)} async-done(((bf16[16,512,64]{1,2,0:T(8,128)(2,1)}), bf16[16,512,64]{1,2,0:T(8,128)(2,1)}) %all-reduce.4.cloned.1.call-update) | async-done | bytes 1048592 | tf_op jit(solution)/shard_map/psum | solution.py:72
  95.5 1.7 fusion.8
  97.2 1.8 fusion.11
  99.0 0.0 copy-start.7
  99.0 0.6 fusion.14
  99.7 0.7 fusion.17
  100.4 0.9 copy.42
  101.2 0.0 reduce-scatter.2.cloned.1.call-update
  101.3 0.0 all-reduce.6.cloned.1.call-start
  101.3 0.0 copy-done.7
  101.3 0.2 multiply_reduce_fusion
  101.5 0.7 dynamic-slice_multiply_fusion.1
  102.2 31.9 %reduce-scatter.2.cloned.1.call-done = bf16[16,1024]{1,0:T(8,128)(2,1)} async-done(((bf16[16,8192]{1,0:T(8,128)(2,1)}), bf16[16,1024]{1,0:T(8,128)(2,1)}) %reduce-scatter.2.cloned.1.call-update) | async-done | bytes 32784 | tf_op jit(solution)/shard_map/reduce_scatter | solution.py:91
  134.1 0.8 fusion.42
  134.9 13.5 %all_gather.3 = bf16[64,1024]{1,0:T(8,128)(2,1)S(1)} all-gather(bf16[16,1024]{1,0:T(8,128)(2,1)S(1)} %fusion.42), channel_id=1, replica_groups=mesh['tp'=8,'dp'=4] {'dp'}, dimensions={0}, use_global_device_ids=true | all-gather | bytes 163840 | tf_op jit(solution)/shard_map/all_gather | solution.py:98
  148.4 0.3 fusion.56
  148.7 0.1 multiply_reduce_fusion.1
  148.8 0.1 broadcast_in_dim.28
  148.9 0.7 pad_maximum_fusion.1
  149.6 0.0 all-reduce.6.cloned.1.call-update
  149.6 52.0 %all-reduce.6.cloned.1.call-done = f32[4,24,384]{2,1,0:T(8,128)} async-done(((f32[4,24,384]{2,1,0:T(8,128)}), f32[4,24,384]{2,1,0:T(8,128)}) %all-reduce.6.cloned.1.call-update) | async-done | bytes 147472 | tf_op jit(solution)/shard_map/psum | solution.py:111
  201.6 4.6 %all-to-all-start = ((f32[4,24,384]{2,1,0:T(8,128)}), f32[4,24,384]{2,1,0:T(8,128)S(1)}, u32[]{:S(2)}, u32[]{:S(2)}) async-start(f32[4,24,384]{2,1,0:T(8,128)} %all-reduce.6.cloned.1.call-done), calls=%async_computation.1 | async-start | bytes 294912 | tf_op jit(solution)/shard_map/all_to_all | solution.py:112
  206.2 6.6 %all-to-all-done = f32[4,24,384]{2,1,0:T(8,128)S(1)} async-done(((f32[4,24,384]{2,1,0:T(8,128)}), f32[4,24,384]{2,1,0:T(8,128)S(1)}, u32[]{:S(2)}, u32[]{:S(2)}) %all-to-all-start) | async-done | bytes 147488 | tf_op jit(solution)/shard_map/all_to_all | solution.py:112
  212.9 0.1 fusion.47
  213.0 0.7 fusion.49
  (21 shorter events, 0.2 us)
Async XLA Ops:
  6.5 0.7 copy-start
  6.5 88.9 %all-reduce.4.cloned.1.call-start = ((), (), s32[]{:S(2)}) async-start(), calls=%async_computation.2 | async-start | bytes 2097152 | tf_op jit(solution)/shard_map/psum | solution.py:72
  18.8 7.2 %copy-start.1 = (bf16[16,512,160]{1,2,0:T(8,128)(2,1)}, bf16[16,512,160]{1,2,0:T(8,128)(2,1)S(1)}, u32[]{:S(2)}) copy-start(bf16[16,512,160]{1,2,0:T(8,128)(2,1)S(1)} %convert_bitcast_fusion) | copy-start | bytes 7864324
  26.0 7.2 %copy-start.3 = (bf16[16,512,144]{1,2,0:T(8,128)(2,1)}, bf16[16,512,144]{1,2,0:T(8,128)(2,1)S(1)}, u32[]{:S(2)}) copy-start(bf16[16,512,144]{1,2,0:T(8,128)(2,1)S(1)} %convert_bitcast_fusion.2) | copy-start | bytes 7077892
  26.1 8.6 %copy-start.8 = (s32[16]{0:T(128)S(1)}, s32[16]{0:T(128)}, u32[]{:S(2)}) copy-start(s32[16]{0:T(128)} %param.14) | copy-start | bytes 196
  26.1 8.6 %slice-start = ((bf16[16,512,160]{1,2,0:T(8,128)(2,1)}), bf16[16,512,32]{1,2,0:T(8,128)(2,1)S(1)}, s32[]{:S(2)}) async-start(bf16[16,512,160]{1,2,0:T(8,128)(2,1)} %copy-done.1), calls=%async_computation.5 | async-start | bytes 1048576 | tf_op jit(solution)/shard_map/slice | solution.py:69
  33.2 1.4 copy-start.5
  33.2 62.3 %copy-start.2 = (bf16[16,512,160]{1,2,0:T(8,128)(2,1)S(1)}, bf16[16,512,160]{1,2,0:T(8,128)(2,1)}, u32[]{:S(2)}) copy-start(bf16[16,512,160]{1,2,0:T(8,128)(2,1)} %copy-done.1) | copy-start | bytes 7864324
  36.0 98.1 %reduce-scatter.2.cloned.1.call-start = ((), (), s32[]{:S(2)}) async-start(), calls=%async_computation.3 | async-start | bytes 294912 | tf_op jit(solution)/shard_map/reduce_scatter | solution.py:91
  95.5 3.5 %copy-start.4 = (bf16[16,512,144]{1,2,0:T(8,128)(2,1)S(1)}, bf16[16,512,144]{1,2,0:T(8,128)(2,1)}, u32[]{:S(2)}) copy-start(bf16[16,512,144]{1,2,0:T(8,128)(2,1)} %copy-done.3) | copy-start | bytes 7077892
  95.5 3.5 %copy-start.9 = (bf16[16,512,64]{1,2,0:T(8,128)(2,1)S(1)}, bf16[16,512,64]{1,2,0:T(8,128)(2,1)}, u32[]{:S(2)}) copy-start(bf16[16,512,64]{1,2,0:T(8,128)(2,1)} %all-reduce.4.cloned.1.call-done) | copy-start | bytes 3145732
  97.2 2.4 %copy-start.6 = (bf16[16,512,144]{1,2,0:T(8,128)(2,1)S(1)}, bf16[16,512,144]{1,2,0:T(8,128)(2,1)}, u32[]{:S(2)}) copy-start(bf16[16,512,144]{1,2,0:T(8,128)(2,1)} %copy-done.5) | copy-start | bytes 7077892
  99.0 2.3 %copy-start.7 = (bf16[256,1024]{1,0:T(8,128)(2,1)S(1)}, bf16[256,1024]{1,0:T(8,128)(2,1)}, u32[]{:S(2)}) copy-start(bf16[256,1024]{1,0:T(8,128)(2,1)} %param.21) | copy-start | bytes 1572868
  101.3 100.4 %all-reduce.6.cloned.1.call-start = ((), (), s32[]{:S(2)}) async-start(), calls=%async_computation.4 | async-start | bytes 294912 | tf_op jit(solution)/shard_map/psum | solution.py:111
  201.6 11.2 %all-to-all-start = ((f32[4,24,384]{2,1,0:T(8,128)}), f32[4,24,384]{2,1,0:T(8,128)S(1)}, u32[]{:S(2)}, u32[]{:S(2)}) async-start(f32[4,24,384]{2,1,0:T(8,128)} %all-reduce.6.cloned.1.call-done), calls=%async_computation.1 | async-start | bytes 294912 | tf_op jit(solution)/shard_map/all_to_all | solution.py:112
Sparse Core Ops, SparseCore 0:
  36.1 59.2 all-reduce.3
  101.4 32.6 reduce-scatter.1
  149.8 51.8 all-reduce.5

commit v2 on v1

v2 whole, which is shorter than its diff:
```python
import functools
import math

import jax
import jax.numpy as jnp
from jax import lax
from jax.experimental import pallas as pl
from jax.experimental.pallas import tpu as pltpu
from jax.sharding import PartitionSpec as P

MESH = pl.DeviceIdType.MESH
F32 = jnp.float32
BF16 = jnp.bfloat16
BATCHES = 2


def mm(a, b, ca=1, cb=0):
    return lax.dot_general(a, b, (((ca,), (cb,)), ((), ())), preferred_element_type=F32)


def kernel(
    nd,
    n,
    x_hbm,
    q_hbm,
    v_hbm,
    len_ref,
    red_ref,
    exp_ref,
    width_ref,
    sketch_ref,
    m1_ref,
    m2_ref,
    t_hbm,
    out_ref,
    x_buf,
    q_buf,
    v_buf,
    t_buf,
    w_buf,
    wide,
    pair_out,
    pair_in,
    mine,
    comb,
    rs_in,
    gath,
    feat_out,
    feat_in,
    upd,
    u_all,
    sq_out,
    sq_in,
    t_out,
    t_in,
    g_out,
    g_in,
    load_sem,
    t_sem,
    pair_s,
    pair_r,
    rs_s,
    rs_r,
    ag_s,
    ag_r,
    fwd_s,
    fwd_r,
    feat_s,
    feat_r,
    u_s,
    u_r,
    sq_s,
    sq_r,
    tn_s,
    tn_r,
    g_s,
    g_r,
):
    d = lax.axis_index("dp")
    c = lax.axis_index("tp")
    chips = n // 2
    chip, core = c // 2, lax.rem(c, 2)
    partner = chip * 2 + 1 - core
    examples, seq, depth = x_buf.shape
    pairs = examples // 2
    ranks = gath.shape[2]
    rc = ranks // 4
    cut = seq // chips
    rows = ranks // n
    own_targets = t_buf.shape[0]
    out_cols = out_ref.shape[1]
    piece = min(own_targets, out_cols)
    halves = own_targets // piece
    slots = out_cols // piece
    per_batch = pairs // BATCHES

    def remote(src, dst, send, recv, dd, cc):
        return pltpu.make_async_remote_copy(
            src_ref=src, dst_ref=dst, send_sem=send, recv_sem=recv, device_id={"dp": dd, "tp": cc}, device_id_type=MESH
        )

    def load(e):
        return [
            pltpu.make_async_copy(src.at[e], dst.at[e], load_sem.at[j, e])
            for j, (src, dst) in enumerate(((x_hbm, x_buf), (q_hbm, q_buf), (v_hbm, v_buf)))
        ]

    def start_loads(i, _):
        for e in ((1 - core) * pairs + i, core * pairs + i):
            for copy in load(e):
                copy.start()
        return 0

    lax.fori_loop(0, pairs, start_loads, 0)
    t_copy = pltpu.make_async_copy(t_hbm, t_buf, t_sem)
    t_copy.start()

    barrier = pltpu.get_barrier_semaphore()
    total = nd * n
    me = d * n + c

    def greet(r, _):
        other = lax.rem(me + r, total)
        pl.semaphore_signal(
            barrier, inc=1, device_id={"dp": other // n, "tp": lax.rem(other, n)}, device_id_type=MESH
        )
        return 0

    lax.fori_loop(1, total, greet, 0)

    sketch = sketch_ref[...]

    def placed(slot):
        row = lax.broadcasted_iota(jnp.int32, (rc, 128), 0)
        col = lax.broadcasted_iota(jnp.int32, (rc, 128), 1)
        return mm(sketch, jnp.where(col == row + slot * rc, 1.0, 0.0).astype(BF16)).astype(BF16)

    w_buf[0, :, :128] = (mm(red_ref[0], placed(2)) + mm(red_ref[1], placed(3))).astype(BF16)
    w_buf[1, :, :128] = mm(exp_ref[0], placed(0), 0, 0).astype(BF16)
    w_buf[2, :, :128] = mm(exp_ref[1], placed(1), 0, 0).astype(BF16)
    w_buf[0, :, 128:] = width_ref[0]
    w_buf[1, :, 128:] = width_ref[1]
    w_buf[2, :, 128:] = width_ref[1]

    pl.semaphore_wait(barrier, total - 1)

    def project(e, out, i):
        for copy in load(e):
            copy.wait()
        narrow = None
        for j, buf in enumerate((x_buf, q_buf, v_buf)):
            res = mm(buf[e], w_buf[j])
            wide[e, :, j * 128 : (j + 1) * 128] = res[:, 128:].astype(BF16)
            narrow = res[:, :128] if narrow is None else narrow + res[:, :128]
        flat = narrow.T[:ranks]
        token = lax.broadcasted_iota(jnp.int32, (ranks, seq), 1)
        flat = jnp.where(token < len_ref[e], flat, 0.0).astype(BF16)
        for q in range(chips):
            out[i, q] = flat[:, q * cut : (q + 1) * cut]

    def pair_copy(i):
        return remote(pair_out.at[i], pair_in.at[i], pair_s.at[i], pair_r.at[i], d, partner)

    def rs_copy(i, r):
        to = lax.rem(chip + r, chips)
        return remote(comb.at[i, to], rs_in.at[i, r], rs_s.at[i, r], rs_r.at[i, r], d, to * 2 + core)

    def ag_copy(i, r, place):
        to = lax.rem(chip + r, chips)
        block = gath.at[core * pairs + i, place]
        return remote(block, block, ag_s.at[i, r], ag_r.at[i, r], d, to * 2 + core)

    def fwd_copy(i, side):
        block = gath.at[side * pairs + i]
        return remote(block, block, fwd_s.at[i], fwd_r.at[i], d, partner)

    def feat_copy(b, r):
        to = lax.rem(c + r, n)
        return remote(feat_out.at[b, to], feat_in.at[b, r], feat_s.at[b, r], feat_r.at[b, r], d, to)

    def home(h):
        return (d * own_targets + h * piece) // out_cols, lax.rem(d * own_targets + h * piece, out_cols) // piece

    def t_copy_out(i, h):
        j, s = home(h)
        return remote(t_out.at[h], t_in.at[s, c], tn_s.at[i, h], tn_r.at[s, c], i, j)

    def g_copy(i, h):
        j, s = home(h)
        return remote(g_out.at[i, h], g_in.at[s, c], g_s.at[i, h], g_r.at[s, c], i, j)

    def scatter_pieces(make, own_in, own_out):
        for i in range(nd):
            for h in range(halves):
                j, s = home(h)
                here = jnp.logical_and(d == i, c == j)

                @pl.when(jnp.logical_not(here))
                def _():
                    make(i, h).start()

                @pl.when(here)
                def _():
                    own_in[s, c] = own_out(i, h)

    def drain_pieces(make):
        for i in range(nd):
            for h in range(halves):
                j, _ = home(h)

                @pl.when(jnp.logical_not(jnp.logical_and(d == i, c == j)))
                def _():
                    make(i, h).wait_send()

    def receive_pieces(buf, send, recv):
        for s in range(slots):
            source = (c * out_cols + s * piece) // own_targets
            for cc in range(n):

                @pl.when(jnp.logical_not(jnp.logical_and(d == source, c == cc)))
                def _():
                    block = buf.at[s, cc]
                    remote(block, block, send.at[0, 0], recv.at[s, cc], source, cc).wait_recv()

    def step(it, _):
        @pl.when(it < pairs)
        def _():
            project((1 - core) * pairs + it, pair_out, it)
            pair_copy(it).start()
            project(core * pairs + it, mine, it)

        @pl.when(jnp.logical_and(it >= 1, it < pairs + 1))
        def _():
            i = it - 1
            pair_copy(i).wait_recv()
            comb[i] = (mine[i].astype(F32) + pair_in[i].astype(F32)).astype(BF16)
            for r in range(1, chips):
                rs_copy(i, r).start()

        @pl.when(jnp.logical_and(it >= 2, it < pairs + 2))
        def _():
            i = it - 2
            whole = comb[i, chip].astype(F32)
            for r in range(1, chips):
                rs_copy(i, r).wait_recv()
                whole = whole + rs_in[i, r].astype(F32)
            gath[core * pairs + i, chip] = whole.astype(BF16)
            for r in range(1, chips):
                ag_copy(i, r, chip).start()

        @pl.when(jnp.logical_and(it >= 3, it < pairs + 3))
        def _():
            i = it - 3
            for r in range(1, chips):
                ag_copy(i, r, lax.rem(chip + chips - r, chips)).wait_recv()
            fwd_copy(i, core).start()

        @pl.when(it >= 4)
        def _():
            i = it - 4
            fwd_copy(i, 1 - core).wait_recv()
            found = []
            for e in (i, pairs + i):
                g = jnp.concatenate([gath[e, q] for q in range(chips)], axis=1)
                found.append(
                    jnp.concatenate(
                        [
                            mm(g[: 2 * rc], wide[e, :, :128]),
                            mm(g[2 * rc : 3 * rc], wide[e, :, 128:256]),
                            mm(g[3 * rc :], wide[e, :, 256:]),
                        ],
                        axis=0,
                    )
                )
            b, place = i // per_batch, lax.rem(i, per_batch)
            for q in range(n):
                feat_out[b, q, place] = jnp.concatenate(
                    [f[q * rows : (q + 1) * rows] for f in found], axis=0
                ).astype(BF16)

            @pl.when(place == per_batch - 1)
            def _():
                for r in range(1, n):
                    feat_copy(b, r).start()

        @pl.when(it == pairs)
        def _():
            t_copy.wait()
            t = t_buf[...].astype(F32)
            norm = jnp.broadcast_to(jnp.sum(t * t, axis=1, keepdims=True), (own_targets, 128)).T
            for h in range(halves):
                t_out[h] = norm[:8, h * piece : (h + 1) * piece]
            scatter_pieces(t_copy_out, t_in, lambda i, h: t_out[h])

        return 0

    lax.fori_loop(0, pairs + 4, step, 0)

    m1, m2 = m1_ref[c], m2_ref[c]
    for b in range(BATCHES):
        f = feat_out[b, c].astype(F32)
        for r in range(1, n):
            feat_copy(b, r).wait_recv()
            f = f + feat_in[b, r].astype(F32)
        for h in range(2):
            fh = f[:, h * rows : (h + 1) * rows]
            new = (0.9 * m1 + 0.1 * fh) / (jnp.sqrt(0.999 * m2 + 0.001 * fh * fh) + 1e-08)
            upd[h, b * per_batch : (b + 1) * per_batch] = new
    squares = None
    for r in range(rows):
        u = jnp.concatenate([upd[0, :, r, :], upd[1, :, r, :]], axis=0).astype(BF16)
        u_all[d, r] = u
        wide_u = u.astype(F32)
        squares = wide_u * wide_u if squares is None else squares + wide_u * wide_u

    def u_copy(r, place):
        to = lax.rem(d + r, nd)
        return remote(u_all.at[place], u_all.at[place], u_s.at[r], u_r.at[r], to, c)

    def sq_copy(r):
        to = lax.rem(c + r, n)
        return remote(sq_out, sq_in.at[r], sq_s.at[r], sq_r.at[r], d, to)

    for r in range(1, nd):
        u_copy(r, d).start()
    sq_out[...] = squares
    for r in range(1, n):
        sq_copy(r).start()
    for r in range(1, nd):
        u_copy(r, lax.rem(d + nd - r, nd)).wait_recv()
    u_rows = jnp.concatenate(
        [jnp.concatenate([u_all[i, r] for r in range(rows)], axis=1) for i in range(nd)], axis=0
    )
    dots = mm(u_rows, t_buf[...], 1, 1).astype(BF16)
    for i in range(nd):
        for h in range(halves):
            g_out[i, h] = dots[i * examples : (i + 1) * examples, h * piece : (h + 1) * piece]
    scatter_pieces(g_copy, g_in, lambda i, h: g_out[i, h])

    for r in range(1, n):
        sq_copy(r).wait_recv()
        squares = squares + sq_in[r]
    row_scale = lax.rsqrt(jnp.sum(squares, axis=1, keepdims=True) + 1e-06) * math.sqrt(ranks * 128)
    receive_pieces(t_in, tn_s, tn_r)
    column_scale = []
    for s in range(slots):
        norm = t_in[s, 0]
        for cc in range(1, n):
            norm = norm + t_in[s, cc]
        column_scale.append(lax.rsqrt(norm[:1] + 1e-06))
    receive_pieces(g_in, g_s, g_r)
    for s in range(slots):
        acc = g_in[s, 0].astype(F32)
        for cc in range(1, n):
            acc = acc + g_in[s, cc].astype(F32)
        out_ref[:, s * piece : (s + 1) * piece] = acc * row_scale * column_scale[s]

    def drain(i, _):
        pair_copy(i).wait_send()
        fwd_copy(i, core).wait_send()
        for r in range(1, chips):
            rs_copy(i, r).wait_send()
            ag_copy(i, r, chip).wait_send()
        return 0

    lax.fori_loop(0, pairs, drain, 0)
    for r in range(1, n):
        for b in range(BATCHES):
            feat_copy(b, r).wait_send()
        sq_copy(r).wait_send()
    for r in range(1, nd):
        u_copy(r, d).wait_send()
    drain_pieces(t_copy_out)
    drain_pieces(g_copy)


def body(nd, n, x, q, v, lengths, reducing, expanding, width, sketch, m1, m2, targets):
    examples, seq, depth = x.shape
    ranks = 4 * sketch.shape[1]
    pairs, chips, rows = examples // 2, n // 2, ranks // n
    cut = seq // chips
    own_targets = targets.shape[0]
    out_cols = own_targets * nd // n
    piece = min(own_targets, out_cols)
    halves, slots = own_targets // piece, out_cols // piece
    dma = pltpu.SemaphoreType.DMA
    anywhere = pl.BlockSpec(memory_space=pl.ANY)
    vmem = pl.BlockSpec(memory_space=pltpu.VMEM)
    smem = pl.BlockSpec(memory_space=pltpu.SMEM)
    per_batch = pairs // BATCHES
    return pl.pallas_call(
        functools.partial(kernel, nd, n),
        out_shape=jax.ShapeDtypeStruct((examples, out_cols), F32),
        in_specs=[anywhere] * 3 + [smem] + [vmem] * 6 + [anywhere],
        out_specs=vmem,
        scratch_shapes=[
            pltpu.VMEM((examples, seq, depth), BF16),
            pltpu.VMEM((examples, seq, depth), BF16),
            pltpu.VMEM((examples, seq, depth), BF16),
            pltpu.VMEM(targets.shape, BF16),
            pltpu.VMEM((3, depth, 256), BF16),
            pltpu.VMEM((examples, seq, 384), BF16),
            pltpu.VMEM((pairs, chips, ranks, cut), BF16),
            pltpu.VMEM((pairs, chips, ranks, cut), BF16),
            pltpu.VMEM((pairs, chips, ranks, cut), BF16),
            pltpu.VMEM((pairs, chips, ranks, cut), BF16),
            pltpu.VMEM((pairs, chips, ranks, cut), BF16),
            pltpu.VMEM((examples, chips, ranks, cut), BF16),
            pltpu.VMEM((BATCHES, n, per_batch, 2 * rows, 128), BF16),
            pltpu.VMEM((BATCHES, n, per_batch, 2 * rows, 128), BF16),
            pltpu.VMEM((2, pairs, rows, 128), F32),
            pltpu.VMEM((nd, rows, examples, 128), BF16),
            pltpu.VMEM((examples, 128), F32),
            pltpu.VMEM((n, examples, 128), F32),
            pltpu.VMEM((halves, 8, piece), F32),
            pltpu.VMEM((slots, n, 8, piece), F32),
            pltpu.VMEM((nd, halves, examples, piece), BF16),
            pltpu.VMEM((slots, n, examples, piece), BF16),
            dma((3, examples)),
            dma,
            dma((pairs,)),
            dma((pairs,)),
            dma((pairs, chips)),
            dma((pairs, chips)),
            dma((pairs, chips)),
            dma((pairs, chips)),
            dma((pairs,)),
            dma((pairs,)),
            dma((BATCHES, n)),
            dma((BATCHES, n)),
            dma((nd,)),
            dma((nd,)),
            dma((n,)),
            dma((n,)),
            dma((nd, halves)),
            dma((slots, n)),
            dma((nd, halves)),
            dma((slots, n)),
        ],
        compiler_params=pltpu.CompilerParams(
            collective_id=0, has_side_effects=True, vmem_limit_bytes=56 * 1024 * 1024
        ),
    )(
        x,
        q,
        v,
        lengths,
        reducing,
        expanding,
        width,
        sketch,
        m1.reshape(n, rows, 128),
        m2.reshape(n, rows, 128),
        targets,
    )


def solution(mesh):
    placed = (
        P("dp", None, "tp"),
        P("dp", None, "tp"),
        P("dp", None, "tp"),
        P("dp"),
        P(None, "tp", None),
        P(None, None, "tp"),
        P(None, "tp", None),
        P(),
        P(),
        P(),
        P("dp", "tp"),
    )
    names = mesh.axis_names
    order = (mesh.shape["dp"], mesh.shape["tp"])
    run = functools.partial(body, *order)
    assert set(names) == {"dp", "tp"}
    return jax.shard_map(run, mesh=mesh, in_specs=placed, out_specs=P("dp", "tp"), check_vma=False)
```

time: 221 us -> 55.6 us (0.25)
  waiting for transfers between devices: 150 us -> 0 us
  Pallas kernels: 0 us -> 52.7 us
  matrix products: 29.7 us -> 0 us
  blocking collectives: 13.5 us -> 0 us
  between operations: 13.3 us -> 0.01 us
  other arithmetic: 4.71 us -> 0 us
  starting transfers between devices: 4.69 us -> 0 us
    psum x2 -> x0, waiting for transfers between devices: 111 us -> none  [the longest x1 59.4 us: body(): narrow = lax.psum(narrow, 'tp')]
    pallas_call x0 -> x1, Pallas kernels: none -> 52.7 us  [body(): pl.pallas_call(functools.partial(kernel, nd, n), out_shape=jax.ShapeDtype...]
    reduce_scatter x1 -> x0, waiting for transfers between devices: 31.9 us -> none  [body(): lax.psum_scatter(own_features.astype(jnp.bfloat16), 'tp', scatter_dimensi...]
    dot_general x12 -> x0, matrix products: 29.7 us -> none  [the longest x3 20.4 us: project(): jnp.einsum('esd,dc->esc', rows, weights, preferred_element_type=jnp.float32)]
    all_gather x1 -> x0, blocking collectives: 13.5 us -> none  [body(): update = lax.all_gather(update, 'dp', axis=0, tiled=True)]
    all_to_all x1 -> x0, waiting for transfers between devices: 6.65 us -> none  [body(): rows = lax.all_to_all(rows, 'dp', split_axis=0, concat_axis=0, tiled=True)]
    all_to_all x1 -> x0, starting transfers between devices: 4.6 us -> none  [body(): rows = lax.all_to_all(rows, 'dp', split_axis=0, concat_axis=0, tiled=True)]
  transfers between devices with their start and end apart: 4 -> 0, of which waited for: 4 -> 0; matrix products, arithmetic and copies ran while one was open for 0% -> 0% of each run, Pallas kernels for 0% -> 0%
where the time goes in v2:
time: 55.6 us; the launch traced here: 55.3 us
  Pallas kernels  52.7 us (95%)
  local copies, waits for them, and re-layouts  2.68 us (5%)
    pallas_call x1, Pallas kernels, body(): pl.pallas_call(functools.partial(kernel, nd, n), out_shape=jax.ShapeDtype...  52.7 us
    unnamed x2, local copies, waits for them, and re-layouts  2.68 us

profile of v2, /device:TPU:0, one launch (start us, length us, event | category | flops | bytes accessed | tf_op | source)
XLA Modules:
  0.0 55.3 jit_solution(3056076522820976166)
XLA Ops:
  0.0 1.4 %copy.12.sketch_ref = bf16[128,16]{1,0:T(8,128)(2,1)} copy(bf16[128,16]{0,1:T(8,128)(2,1)} %param.18) | data formatting | bytes 8192 | tf_op args[7]
  1.4 52.7 %shard_map.109 = f32[16,128]{1,0:T(8,128)} custom-call(bf16[16,512,512]{2,1,0:T(8,128)(2,1)} %x_hbm.1, bf16[16,512,512]{2,1,0:T(8,128)(2,1)} %q_hbm.1, bf16[16,512,512]{2,1,0:T(8,128)(2,1)} %v_hbm.1, s32[16]{0:T(128)} %len_ref.1, bf16[2,512,128]{2,1,0:T(8,128)(2,1)} %red_ref.1, bf16[2,128,512]{2,1,0:T(8,128)(2,1)} %exp_ref.1, ...), custom_call_target="tpu_custom_call" | custom-call | tf_op jit(solution)/shard_map/pallas_call | solution.py:391
  54.0 1.3 %copy.14 = f32[16,128]{1,0:T(8,128)} copy(f32[16,128]{1,0:T(8,128)} %shard_map.109) | data formatting | bytes 16384

commit v3 on v2

--- a/solution.py
+++ b/solution.py
@@ -25,9 +25,9 @@
     q_hbm,
     v_hbm,
     len_ref,
-    red_ref,
-    exp_ref,
-    width_ref,
+    red_hbm,
+    exp_hbm,
+    width_hbm,
     sketch_ref,
     m1_ref,
     m2_ref,
@@ -37,6 +37,9 @@
     q_buf,
     v_buf,
     t_buf,
+    red_ref,
+    exp_ref,
+    width_ref,
     w_buf,
     wide,
     pair_out,
@@ -57,6 +60,7 @@
     g_in,
     load_sem,
     t_sem,
+    fixed_sem,
     pair_s,
     pair_r,
     rs_s,
@@ -83,9 +87,9 @@
     partner = chip * 2 + 1 - core
     examples, seq, depth = x_buf.shape
     pairs = examples // 2
-    ranks = gath.shape[2]
-    rc = ranks // 4
-    cut = seq // chips
+    rc = sketch_ref.shape[0]
+    ranks = 4 * rc
+    half = seq // 2
     rows = ranks // n
     own_targets = t_buf.shape[0]
     out_cols = out_ref.shape[1]
@@ -111,6 +115,12 @@
                 copy.start()
         return 0
 
+    fixed = [
+        pltpu.make_async_copy(src, dst, fixed_sem.at[j])
+        for j, (src, dst) in enumerate(((red_hbm, red_ref), (exp_hbm, exp_ref), (width_hbm, width_ref)))
+    ]
+    for copy in fixed:
+        copy.start()
     lax.fori_loop(0, pairs, start_loads, 0)
     t_copy = pltpu.make_async_copy(t_hbm, t_buf, t_sem)
     t_copy.start()
@@ -129,11 +139,14 @@
     lax.fori_loop(1, total, greet, 0)
 
     sketch = sketch_ref[...]
+    for copy in fixed:
+        copy.wait()
 
     def placed(slot):
         row = lax.broadcasted_iota(jnp.int32, (rc, 128), 0)
         col = lax.broadcasted_iota(jnp.int32, (rc, 128), 1)
-        return mm(sketch, jnp.where(col == row + slot * rc, 1.0, 0.0).astype(BF16)).astype(BF16)
+        here = jnp.logical_or(col == row + slot * rc, col == row + slot * rc + ranks)
+        return mm(sketch, jnp.where(here, 1.0, 0.0).astype(BF16), 0, 0).astype(BF16)
 
     w_buf[0, :, :128] = (mm(red_ref[0], placed(2)) + mm(red_ref[1], placed(3))).astype(BF16)
     w_buf[1, :, :128] = mm(exp_ref[0], placed(0), 0, 0).astype(BF16)
@@ -147,16 +160,22 @@
     def project(e, out, i):
         for copy in load(e):
             copy.wait()
-        narrow = None
-        for j, buf in enumerate((x_buf, q_buf, v_buf)):
-            res = mm(buf[e], w_buf[j])
-            wide[e, :, j * 128 : (j + 1) * 128] = res[:, 128:].astype(BF16)
-            narrow = res[:, :128] if narrow is None else narrow + res[:, :128]
-        flat = narrow.T[:ranks]
-        token = lax.broadcasted_iota(jnp.int32, (ranks, seq), 1)
-        flat = jnp.where(token < len_ref[e], flat, 0.0).astype(BF16)
-        for q in range(chips):
-            out[i, q] = flat[:, q * cut : (q + 1) * cut]
+        row = lax.broadcasted_iota(jnp.int32, (half, 128), 0)
+        upper = lax.broadcasted_iota(jnp.int32, (half, 128), 1) >= ranks
+        live = jnp.where(upper, row + half, row) < len_ref[e]
+        for k in range(half // 128):
+            sums = []
+            for late in range(2):
+                span = pl.ds(late * half + k * 128, 128)
+                narrow = None
+                for j, buf in enumerate((x_buf, q_buf, v_buf)):
+                    res = mm(buf[e, span], w_buf[j])
+                    wide[e, span, j * 128 : (j + 1) * 128] = res[:, 128:].astype(BF16)
+                    narrow = res[:, :128] if narrow is None else narrow + res[:, :128]
+                sums.append(narrow)
+            packed = jnp.where(upper[:128], sums[1], sums[0])
+            packed = jnp.where(live[k * 128 : (k + 1) * 128], packed, 0.0).astype(BF16)
+            out[i, :, :, k * 128 : (k + 1) * 128] = packed.T.reshape(chips, 128 // chips, 128)
 
     def pair_copy(i):
         return remote(pair_out.at[i], pair_in.at[i], pair_s.at[i], pair_r.at[i], d, partner)
@@ -261,12 +280,14 @@
             fwd_copy(i, 1 - core).wait_recv()
             found = []
             for e in (i, pairs + i):
-                g = jnp.concatenate([gath[e, q] for q in range(chips)], axis=1)
+                g = gath[e].reshape(128, half)
+                g = jnp.concatenate([g[:ranks], g[ranks:]], axis=1)
+                left = mm(g, wide[e, :, :256])
                 found.append(
                     jnp.concatenate(
                         [
-                            mm(g[: 2 * rc], wide[e, :, :128]),
-                            mm(g[2 * rc : 3 * rc], wide[e, :, 128:256]),
+                            left[: 2 * rc, :128],
+                            left[2 * rc : 3 * rc, 128:],
                             mm(g[3 * rc :], wide[e, :, 256:]),
                         ],
                         axis=0,
@@ -378,7 +399,6 @@
     examples, seq, depth = x.shape
     ranks = 4 * sketch.shape[1]
     pairs, chips, rows = examples // 2, n // 2, ranks // n
-    cut = seq // chips
     own_targets = targets.shape[0]
     out_cols = own_targets * nd // n
     piece = min(own_targets, out_cols)
@@ -391,21 +411,24 @@
     return pl.pallas_call(
         functools.partial(kernel, nd, n),
         out_shape=jax.ShapeDtypeStruct((examples, out_cols), F32),
-        in_specs=[anywhere] * 3 + [smem] + [vmem] * 6 + [anywhere],
+        in_specs=[anywhere] * 3 + [smem] + [anywhere] * 3 + [vmem] * 3 + [anywhere],
         out_specs=vmem,
         scratch_shapes=[
             pltpu.VMEM((examples, seq, depth), BF16),
             pltpu.VMEM((examples, seq, depth), BF16),
             pltpu.VMEM((examples, seq, depth), BF16),
             pltpu.VMEM(targets.shape, BF16),
+            pltpu.VMEM(reducing.shape, BF16),
+            pltpu.VMEM(expanding.shape, BF16),
+            pltpu.VMEM(width.shape, BF16),
             pltpu.VMEM((3, depth, 256), BF16),
             pltpu.VMEM((examples, seq, 384), BF16),
-            pltpu.VMEM((pairs, chips, ranks, cut), BF16),
-            pltpu.VMEM((pairs, chips, ranks, cut), BF16),
-            pltpu.VMEM((pairs, chips, ranks, cut), BF16),
-            pltpu.VMEM((pairs, chips, ranks, cut), BF16),
-            pltpu.VMEM((pairs, chips, ranks, cut), BF16),
-            pltpu.VMEM((examples, chips, ranks, cut), BF16),
+            pltpu.VMEM((pairs, chips, 128 // chips, seq // 2), BF16),
+            pltpu.VMEM((pairs, chips, 128 // chips, seq // 2), BF16),
+            pltpu.VMEM((pairs, chips, 128 // chips, seq // 2), BF16),
+            pltpu.VMEM((pairs, chips, 128 // chips, seq // 2), BF16),
+            pltpu.VMEM((pairs, chips, 128 // chips, seq // 2), BF16),
+            pltpu.VMEM((examples, chips, 128 // chips, seq // 2), BF16),
             pltpu.VMEM((BATCHES, n, per_batch, 2 * rows, 128), BF16),
             pltpu.VMEM((BATCHES, n, per_batch, 2 * rows, 128), BF16),
             pltpu.VMEM((2, pairs, rows, 128), F32),
@@ -418,6 +441,7 @@
             pltpu.VMEM((slots, n, examples, piece), BF16),
             dma((3, examples)),
             dma,
+            dma((3,)),
             dma((pairs,)),
             dma((pairs,)),
             dma((pairs, chips)),
@@ -448,7 +472,7 @@
         reducing,
         expanding,
         width,
-        sketch,
+        sketch.T,
         m1.reshape(n, rows, 128),
         m2.reshape(n, rows, 128),
         targets,

time: 55.6 us -> 53 us (0.953)
  local copies, waits for them, and re-layouts: 2.68 us -> 1.3 us
  Pallas kernels: 52.7 us -> 51.5 us
    unnamed x2 -> x1, local copies, waits for them, and re-layouts: 2.68 us -> 1.3 us
    pallas_call x1, Pallas kernels: 52.7 us -> 51.5 us  [body(): pl.pallas_call(functools.partial(kernel, nd, n), out_shape=jax.ShapeDtype...]
where the time goes in v3:
time: 53 us; the launch traced here: 52.8 us
  Pallas kernels  51.5 us (97%)
  local copies, waits for them, and re-layouts  1.3 us (2%)
    pallas_call x1, Pallas kernels, body(): pl.pallas_call(functools.partial(kernel, nd, n), out_shape=jax.ShapeDtype...  51.5 us
    unnamed x1, local copies, waits for them, and re-layouts  1.3 us

profile of v3, /device:TPU:0, one launch (start us, length us, event | category | flops | bytes accessed | tf_op | source)
XLA Modules:
  0.0 52.8 jit_solution(270384773734523996)
XLA Ops:
  0.0 51.5 %shard_map.109 = f32[16,128]{1,0:T(8,128)} custom-call(bf16[16,512,512]{2,1,0:T(8,128)(2,1)} %x_hbm.1, bf16[16,512,512]{2,1,0:T(8,128)(2,1)} %q_hbm.1, bf16[16,512,512]{2,1,0:T(8,128)(2,1)} %v_hbm.1, s32[16]{0:T(128)} %len_ref.1, bf16[2,512,128]{2,1,0:T(8,128)(2,1)} %red_hbm.1, bf16[2,128,512]{2,1,0:T(8,128)(2,1)} %exp_hbm.1, ...), custom_call_target="tpu_custom_call" | custom-call | tf_op jit(solution)/shard_map/pallas_call | solution.py:411
  51.5 1.3 %copy.13 = f32[16,128]{1,0:T(8,128)} copy(f32[16,128]{1,0:T(8,128)} %shard_map.109) | data formatting | bytes 16384
